TPU v7x, 32 devices: a whole 2x2x4 slice. The times are simulated.
32 devices in a mesh: row: 4 (over y, x), col: 8 (over z, core).
Axes of the slice: x: 2, y: 2, z: 4, core: 2. Of those that a mesh axis runs over, the one named last changes fastest.
Arguments:
- amplitudes: bfloat16 [4096, 16384], P('col', 'row'), may hold values from -6 to 6
- integrals: bfloat16 [4096, 16384], P('row', 'col'), may hold values from -0.09375 to 0.09375
- tile_mask: int32 [64, 256], P(None, 'row'), may hold values from 0 to 1, as said below
- occ_energy: float32 [4], replicated, may hold values from -1 to -0.2
- virt_energy: float32 [4096], replicated, may hold values from 0.2 to 1.5
Outputs:
- update: bfloat16 [16384, 16384], P(('row', 'col'))
Inputs may be any that keep to these rules, and one draw needn't show every extreme that they name: `tile_mask`: 0 drops a tile, 1 keeps it; the share of kept tiles differs strongly between groups of (ia) rows.
All inputs are finite; a program needn't handle non-finite values.
Results may differ from a plain program's by a relative error of at most 0.0049.
Values may be sent and summed in bfloat16 or wider, within the bound.
A program may use at most 192 MiB of HBM per device.

v0:
```python
import jax
import jax.numpy as jnp
from jax import lax
from jax.sharding import PartitionSpec as P

TILE = 64


def local(amplitudes, integrals, tile_mask, occ_energy, virt_energy):
    col_count = lax.axis_size("col")
    row_place = lax.axis_index("row")
    col_place = lax.axis_index("col")
    local_depth, local_width = amplitudes.shape
    tile_rows = local_depth // TILE
    tile_cols = local_width // TILE
    own_mask = lax.dynamic_slice_in_dim(tile_mask, col_place * tile_rows, tile_rows, 0)
    keep_tiles = own_mask.astype(jnp.bfloat16)
    masked = (
        amplitudes.reshape(tile_rows, TILE, tile_cols, TILE) * keep_tiles[:, None, :, None]
    ).reshape(local_depth, local_width)
    whole_panel = lax.all_gather(integrals, "row", axis=0, tiled=True)
    left_rows = lax.all_gather(masked, "col", axis=0, tiled=True)
    product_block = lax.dot_general(
        left_rows, whole_panel, (((0,), (0,)), ((), ())), preferred_element_type=jnp.float32
    )
    cycle_block = product_block.astype(jnp.bfloat16)
    flat_rows = lax.all_to_all(cycle_block, "col", split_axis=0, concat_axis=1, tiled=True)
    rows_here, total_cols = flat_rows.shape
    pieces = total_cols // rows_here
    arrived = lax.all_to_all(
        flat_rows.reshape(rows_here, pieces, rows_here),
        ("row", "col"),
        split_axis=1,
        concat_axis=1,
        tiled=True,
    )
    mirrored = jnp.transpose(arrived, (2, 1, 0)).reshape(rows_here, total_cols)
    pair_gap = (virt_energy[None, :] - occ_energy[:, None]).reshape(total_cols)
    flat_place = row_place * col_count + col_place
    row_gap = lax.dynamic_slice_in_dim(pair_gap, flat_place * rows_here, rows_here, 0)
    summed = flat_rows.astype(jnp.float32) + mirrored.astype(jnp.float32)
    return (summed / (row_gap[:, None] + pair_gap[None, :])).astype(jnp.bfloat16)


def solution(mesh):
    return jax.shard_map(
        local,
        mesh=mesh,
        in_specs=(P("col", "row"), P("row", "col"), P(None, "row"), P(), P()),
        out_specs=P(("row", "col"), None),
        check_vma=False,
    )
```

profile of v0, /device:TPU:0, one launch (start us, length us, event | category | flops | bytes accessed | tf_op | source)
XLA Modules:
  0.0 1402.9 jit_solution(14816292952681816901)
XLA Ops:
  6.5 0.0 all-gather.5.cloned.1.call-start
  6.5 0.7 all-gather.5.cloned.1.call-update
  7.3 0.0 all-gather.3.cloned.1.call-start
  7.3 0.7 dynamic-slice_convert_fusion
  8.0 5.6 mul.21
  13.6 12.6 mul.22
  26.3 7.9 mul.23
  34.1 0.0 all-gather.3.cloned.1.call-update
  34.2 135.1 %all-gather.5.cloned.1.call-done = bf16[4096,2048]{1,0:T(8,128)(2,1)} async-done(((bf16[1024,2048]{1,0:T(8,128)(2,1)}), bf16[4096,2048]{1,0:T(8,128)(2,1)}) %all-gather.5.cloned.1.call-update) | async-done | bytes 16777232 | tf_op jit(solution)/shard_map/all_gather | solution.py:21
  169.2 290.2 %all-gather.3.cloned.1.call-done = bf16[4096,4096]{1,0:T(8,128)(2,1)} async-done(((bf16[512,4096]{1,0:T(8,128)(2,1)}), bf16[4096,4096]{1,0:T(8,128)(2,1)}) %all-gather.3.cloned.1.call-update) | async-done | bytes 33554448 | tf_op jit(solution)/shard_map/all_gather | solution.py:22
  459.4 79.4 %convolution_convert_fusion = bf16[4096,2048]{1,0:T(8,128)(2,1)} fusion(bf16[4096,4096]{1,0:T(8,128)(2,1)} %all-gather.3.cloned.1.call-done, bf16[4096,2048]{1,0:T(8,128)(2,1)} %all-gather.5.cloned.1.call-done), kind=kOutput, calls=%fused_computation.4 | convolution fusion | flops 68727865344 | bytes 67108864 | tf_op jit(solution)/shard_map/dot_general | solution.py:23
  538.9 21.6 %copy.9 = bf16[8,512,2048]{1,2,0:T(8,128)(2,1)} copy(bf16[8,512,2048]{2,1,0:T(8,128)(2,1)} %bitcast.20) | data formatting | bytes 33554432 | tf_op jit(solution)/shard_map/all_to_all | solution.py:27
  560.5 371.1 %all_to_all.21 = bf16[8,512,2048]{1,2,0:T(8,128)(2,1)} all-to-all(bf16[8,512,2048]{1,2,0:T(8,128)(2,1)} %copy.9), channel_id=1, replica_groups=mesh['row'=4,'col'=8] {'col'}, dimensions={0} | all-to-all | bytes 33554432 | tf_op jit(solution)/shard_map/all_to_all | solution.py:27
  931.6 0.0 copy-start
  931.6 0.0 copy-start.1
  931.6 4.0 all-to-all-start.1
  935.7 0.0 copy-done
  935.7 0.0 copy-done.1
  935.7 0.1 subtract_bitcast_fusion
  935.8 0.1 dynamic_slice.7
  935.9 364.4 %all-to-all-done.1 = bf16[512,32,512]{0,2,1:T(8,128)(2,1)} async-done(((bf16[512,32,512]{0,2,1:T(8,128)(2,1)}), bf16[512,32,512]{0,2,1:T(8,128)(2,1)}, u32[]{:S(2)}, u32[]{:S(2)}) %all-to-all-start.1) | async-done | bytes 16777248 | tf_op jit(solution)/shard_map/all_to_all | solution.py:30
  1300.2 18.8 %convert_bitcast_fusion = f32[512,32,512]{2,0,1:T(8,128)} fusion(bf16[512,32,512]{0,2,1:T(8,128)(2,1)} %all-to-all-done.1), kind=kLoop, calls=%fused_computation.3 | loop fusion | flops 8388608 | bytes 50331648 | tf_op jit(solution)/shard_map/convert_element_type | solution.py:41
  1319.0 33.4 %copy.10 = f32[512,32,512]{0,2,1:T(8,128)} copy(f32[512,32,512]{2,0,1:T(8,128)} %convert_bitcast_fusion) | data formatting | bytes 67108864 | tf_op jit(solution)/shard_map/convert_element_type | solution.py:41
  1352.4 22.5 %fusion.1 = bf16[512,16384]{0,1:T(8,128)(2,1)} fusion(f32[512,32,512]{0,2,1:T(8,128)} %copy.10, bf16[8,512,2048]{1,2,0:T(8,128)(2,1)} %all_to_all.21, f32[16384]{0:T(1024)S(1)} %bitcast.22, f32[512]{0:T(512)S(1)} %dynamic_slice.7), kind=kLoop, calls=%fused_computation.2 | loop fusion | flops 41943040 | bytes 67176448 | tf_op jit(solution)/shard_map/convert_element_type | solution.py:42
  1374.9 21.2 %copy.11 = bf16[512,16384]{1,0:T(8,128)(2,1)} copy(bf16[512,16384]{0,1:T(8,128)(2,1)} %fusion.1) | data formatting | bytes 33554432 | tf_op jit(solution)/shard_map/convert_element_type | solution.py:42
  (1 shorter events, 0.0 us)
Async XLA Ops:
  6.5 162.7 %all-gather.5.cloned.1.call-start = ((), (), s32[]{:S(2)}) async-start(), calls=%async_computation.3 | async-start | bytes 20971520 | tf_op jit(solution)/shard_map/all_gather | solution.py:21
  7.3 452.2 %all-gather.3.cloned.1.call-start = ((), (), s32[]{:S(2)}) async-start(), calls=%async_computation.2 | async-start | bytes 37748736 | tf_op jit(solution)/shard_map/all_gather | solution.py:22
  931.6 4.0 copy-start
  931.6 4.0 copy-start.1
  931.6 368.6 %all-to-all-start.1 = ((bf16[512,32,512]{0,2,1:T(8,128)(2,1)}), bf16[512,32,512]{0,2,1:T(8,128)(2,1)}, u32[]{:S(2)}, u32[]{:S(2)}) async-start(bf16[512,32,512]{0,2,1:T(8,128)(2,1)} %bitcast.19), calls=%async_computation.1 | async-start | bytes 33554432 | tf_op jit(solution)/shard_map/all_to_all | solution.py:30
Sparse Core Ops, SparseCore 0:
  9.2 160.0 all-gather.4
  170.8 288.5 all-gather.2
where the time goes:
time: 1410 us; the launch traced here: 1400 us
  waiting for transfers between devices  790 us (56%)
  blocking collectives  371 us (26%)
  local copies, waits for them, and re-layouts  94.5 us (7%)
  matrix products  79.4 us (6%)
  other arithmetic  50 us (4%)
    all_to_all x1, blocking collectives, local(): lax.all_to_all(cycle_block, 'col', split_axis=0, concat_axis=1, tiled=True)  371 us
    all_to_all x1, waiting for transfers between devices, local(): lax.all_to_all(flat_rows.reshape(rows_here, pieces, rows_here), ('row', '...  364 us
    all_gather x1, waiting for transfers between devices, local(): left_rows = lax.all_gather(masked, 'col', axis=0, tiled=True)  290 us
    all_gather x1, waiting for transfers between devices, local(): whole_panel = lax.all_gather(integrals, 'row', axis=0, tiled=True)  135 us
    dot_general x1, matrix products, local(): lax.dot_general(left_rows, whole_panel, (((0,), (0,)), ((), ())), preferr...  79.4 us
    convert_element_type x1, local copies, waits for them, and re-layouts, local(): summed = flat_rows.astype(jnp.float32) + mirrored.astype(jnp.float32)  33.4 us
  transfers between devices with their start and end apart: 3, of which 3 were waited for; matrix products, arithmetic and copies ran while one was open for 2% of the time, Pallas kernels for 0%

commit v1 on v0

--- a/solution.py
+++ b/solution.py
@@ -4,6 +4,24 @@
 from jax.sharding import PartitionSpec as P
 
 TILE = 64
+
+
+def gather_around(shard, axis, dim):
+    ways, here, lap = (lax.axis_size(axis), lax.axis_index(axis), shard.shape[dim])
+    shape = [n * ways if d == dim else n for d, n in enumerate(shard.shape)]
+    full = lax.dynamic_update_slice_in_dim(
+        jnp.zeros(shape, shard.dtype), shard, here * lap, axis=dim
+    )
+    going_up = going_down = shard
+    for far in range(1, ways // 2 + 1):
+        going_up = lax.ppermute(going_up, axis, [(d, (d + 1) % ways) for d in range(ways)])
+        full = lax.dynamic_update_slice_in_dim(full, going_up, (here - far) % ways * lap, axis=dim)
+        if 2 * far < ways:
+            going_down = lax.ppermute(going_down, axis, [(d, (d - 1) % ways) for d in range(ways)])
+            full = lax.dynamic_update_slice_in_dim(
+                full, going_down, (here + far) % ways * lap, axis=dim
+            )
+    return full
 
 
 def local(amplitudes, integrals, tile_mask, occ_energy, virt_energy):
@@ -18,7 +36,7 @@
     masked = (
         amplitudes.reshape(tile_rows, TILE, tile_cols, TILE) * keep_tiles[:, None, :, None]
     ).reshape(local_depth, local_width)
-    whole_panel = lax.all_gather(integrals, "row", axis=0, tiled=True)
+    whole_panel = gather_around(integrals, "row", 0)
     left_rows = lax.all_gather(masked, "col", axis=0, tiled=True)
     product_block = lax.dot_general(
         left_rows, whole_panel, (((0,), (0,)), ((), ())), preferred_element_type=jnp.float32

time: 1410 us -> 1270 us (0.901)
  waiting for transfers between devices: 790 us -> 627 us
  local copies, waits for them, and re-layouts: 94.5 us -> 118 us
    all_gather x1, waiting for transfers between devices: 290 us -> 12.1 us  [local(): left_rows = lax.all_gather(masked, 'col', axis=0, tiled=True)]
    ppermute x0 -> x3, waiting for transfers between devices: none -> 251 us  [the longest x2 175 us: gather_around(): lax.ppermute(going_up, axis, [(d, (d + 1) % ways) for d in range(ways)])]
    all_gather x1 -> x0, waiting for transfers between devices: 135 us -> none  [local(): whole_panel = lax.all_gather(integrals, 'row', axis=0, tiled=True)]
    dynamic_update_slice x0 -> x4, local copies, waits for them, and re-layouts: none -> 16.9 us  [the longest x2 9.57 us: gather_around(): lax.dynamic_update_slice_in_dim(full, going_up, (here - far) % ways * lap...]
  transfers between devices with their start and end apart: 3 -> 5, of which waited for: 3 -> 5; matrix products, arithmetic and copies ran while one was open for 2% -> 2% of each run, Pallas kernels for 0% -> 0%
where the time goes in v1:
time: 1270 us
  waiting for transfers between devices  627 us (49%)
  blocking collectives  371 us (29%)
  local copies, waits for them, and re-layouts  118 us (9%)
  matrix products  79.5 us (6%)
  other arithmetic  49.3 us (4%)
  between operations  13.4 us (1%)
    all_to_all x1, blocking collectives, local(): lax.all_to_all(cycle_block, 'col', split_axis=0, concat_axis=1, tiled=True)  371 us
    all_to_all x1, waiting for transfers between devices, local(): lax.all_to_all(flat_rows.reshape(rows_here, pieces, rows_here), ('row', '...  364 us
    ppermute x2, waiting for transfers between devices, gather_around(): lax.ppermute(going_up, axis, [(d, (d + 1) % ways) for d in range(ways)])  175 us
    dot_general x1, matrix products, local(): lax.dot_general(left_rows, whole_panel, (((0,), (0,)), ((), ())), preferr...  79.5 us
    ppermute x1, waiting for transfers between devices, gather_around(): lax.ppermute(going_down, axis, [(d, (d - 1) % ways) for d in range(ways)])  75.4 us
    convert_element_type x1, local copies, waits for them, and re-layouts, local(): summed = flat_rows.astype(jnp.float32) + mirrored.astype(jnp.float32)  33.4 us
  transfers between devices with their start and end apart: 5, of which 5 were waited for; matrix products, arithmetic and copies ran while one was open for 2% of the time, Pallas kernels for 0%

profile of v1, /device:TPU:0, one launch (start us, length us, event | category | flops | bytes accessed | tf_op | source)
XLA Modules:
  0.0 1267.1 jit_solution(10143293611574722081)
XLA Ops:
  6.5 0.0 all-gather.2.cloned.1.call-start
  6.5 0.7 dynamic-slice_convert_fusion
  7.2 5.6 mul.33
  12.8 12.0 mul.34
  24.9 7.2 mul.35
  32.0 0.0 all-gather.2.cloned.1.call-update
  32.1 3.0 collective-permute-start
  35.1 1.0 collective-permute-start.1
  36.1 91.7 %collective-permute-done = bf16[1024,2048]{1,0:T(8,128)(2,1)} collective-permute-done((bf16[1024,2048]{1,0:T(8,128)(2,1)}, bf16[1024,2048]{1,0:T(8,128)(2,1)}, u32[]{:S(2)}, u32[]{:S(2)}) %collective-permute-start) | collective-permute-done | bytes 4194336 | tf_op jit(solution)/shard_map/ppermute | solution.py:17
  127.8 1.1 collective-permute-start.2
  128.8 0.0 copy-start
  128.8 6.8 broadcast_in_dim.2
  135.7 0.0 copy-done
  135.7 2.3 constant_dynamic-update-slice_fusion.3
  138.0 4.8 constant_dynamic-update-slice_fusion.2
  142.8 75.4 %collective-permute-done.1 = bf16[1024,2048]{1,0:T(8,128)(2,1)} collective-permute-done((bf16[1024,2048]{1,0:T(8,128)(2,1)}, bf16[1024,2048]{1,0:T(8,128)(2,1)}, u32[]{:S(2)}, u32[]{:S(2)}) %collective-permute-start.1) | collective-permute-done | bytes 4194336 | tf_op jit(solution)/shard_map/ppermute | solution.py:20
  218.2 5.0 constant_dynamic-update-slice_fusion.1
  223.2 83.5 %collective-permute-done.2 = bf16[1024,2048]{1,0:T(8,128)(2,1)} collective-permute-done((bf16[1024,2048]{1,0:T(8,128)(2,1)}, bf16[1024,2048]{1,0:T(8,128)(2,1)}, u32[]{:S(2)}, u32[]{:S(2)}) %collective-permute-start.2) | collective-permute-done | bytes 4194336 | tf_op jit(solution)/shard_map/ppermute | solution.py:17
  306.7 4.8 constant_dynamic-update-slice_fusion
  311.5 12.1 all-gather.2.cloned.1.call-done
  323.5 79.5 %convolution_convert_fusion = bf16[4096,2048]{1,0:T(8,128)(2,1)} fusion(bf16[4096,4096]{1,0:T(8,128)(2,1)} %all-gather.2.cloned.1.call-done, bf16[4096,2048]{1,0:T(8,128)(2,1)} %constant_dynamic-update-slice_fusion), kind=kOutput, calls=%fused_computation.4 | convolution fusion | flops 68727865344 | bytes 67108864 | tf_op jit(solution)/shard_map/dot_general | solution.py:41
  403.1 21.5 %copy.9 = bf16[8,512,2048]{1,2,0:T(8,128)(2,1)} copy(bf16[8,512,2048]{2,1,0:T(8,128)(2,1)} %bitcast.20) | data formatting | bytes 33554432 | tf_op jit(solution)/shard_map/all_to_all | solution.py:45
  424.6 371.2 %all_to_all.21 = bf16[8,512,2048]{1,2,0:T(8,128)(2,1)} all-to-all(bf16[8,512,2048]{1,2,0:T(8,128)(2,1)} %copy.9), channel_id=1, replica_groups=mesh['row'=4,'col'=8] {'col'}, dimensions={0} | all-to-all | bytes 33554432 | tf_op jit(solution)/shard_map/all_to_all | solution.py:45
  795.8 0.0 copy-start.1
  795.8 0.0 copy-start.2
  795.8 4.0 all-to-all-start.1
  799.8 0.0 copy-done.1
  799.8 0.0 copy-done.2
  799.8 0.1 subtract_bitcast_fusion
  799.9 0.1 dynamic_slice.7
  800.0 364.3 %all-to-all-done.1 = bf16[512,32,512]{0,2,1:T(8,128)(2,1)} async-done(((bf16[512,32,512]{0,2,1:T(8,128)(2,1)}), bf16[512,32,512]{0,2,1:T(8,128)(2,1)}, u32[]{:S(2)}, u32[]{:S(2)}) %all-to-all-start.1) | async-done | bytes 16777248 | tf_op jit(solution)/shard_map/all_to_all | solution.py:48
  1164.3 18.8 %convert_bitcast_fusion = f32[512,32,512]{2,0,1:T(8,128)} fusion(bf16[512,32,512]{0,2,1:T(8,128)(2,1)} %all-to-all-done.1), kind=kLoop, calls=%fused_computation.3 | loop fusion | flops 8388608 | bytes 50331648 | tf_op jit(solution)/shard_map/convert_element_type | solution.py:59
  1183.2 33.4 %copy.10 = f32[512,32,512]{0,2,1:T(8,128)} copy(f32[512,32,512]{2,0,1:T(8,128)} %convert_bitcast_fusion) | data formatting | bytes 67108864 | tf_op jit(solution)/shard_map/convert_element_type | solution.py:59
  1216.5 22.5 %fusion.1 = bf16[512,16384]{0,1:T(8,128)(2,1)} fusion(f32[512,32,512]{0,2,1:T(8,128)} %copy.10, bf16[8,512,2048]{1,2,0:T(8,128)(2,1)} %all_to_all.21, f32[16384]{0:T(1024)S(1)} %bitcast.22, f32[512]{0:T(512)S(1)} %dynamic_slice.7), kind=kLoop, calls=%fused_computation.2 | loop fusion | flops 41943040 | bytes 67176448 | tf_op jit(solution)/shard_map/convert_element_type | solution.py:60
  1239.1 21.2 %copy.11 = bf16[512,16384]{1,0:T(8,128)(2,1)} copy(bf16[512,16384]{0,1:T(8,128)(2,1)} %fusion.1) | data formatting | bytes 33554432 | tf_op jit(solution)/shard_map/convert_element_type | solution.py:60
  (1 shorter events, 0.0 us)
Async XLA Ops:
  6.5 317.0 %all-gather.2.cloned.1.call-start = ((), (), s32[]{:S(2)}) async-start(), calls=%async_computation.2 | async-start | bytes 37748736 | tf_op jit(solution)/shard_map/all_gather | solution.py:40
  32.1 95.7 %collective-permute-start = (bf16[1024,2048]{1,0:T(8,128)(2,1)}, bf16[1024,2048]{1,0:T(8,128)(2,1)}, u32[]{:S(2)}, u32[]{:S(2)}) collective-permute-start(bf16[1024,2048]{1,0:T(8,128)(2,1)} %param.6), channel_id=1, source_target_pairs={{0,8},{8,16},{16,24},{24,0},{1,9},{9,17},{17,25},{25,1},{2,10},{10... | collective-permute-start | bytes 12582920 | tf_op jit(solution)/shard_map/ppermute | solution.py:17
  35.1 183.1 %collective-permute-start.1 = (bf16[1024,2048]{1,0:T(8,128)(2,1)}, bf16[1024,2048]{1,0:T(8,128)(2,1)}, u32[]{:S(2)}, u32[]{:S(2)}) collective-permute-start(bf16[1024,2048]{1,0:T(8,128)(2,1)} %param.6), channel_id=1, source_target_pairs={{0,24},{8,0},{16,8},{24,16},{1,25},{9,1},{17,9},{25,17},{2,26},{10... | collective-permute-start | bytes 12582920 | tf_op jit(solution)/shard_map/ppermute | solution.py:20
  127.8 178.9 %collective-permute-start.2 = (bf16[1024,2048]{1,0:T(8,128)(2,1)}, bf16[1024,2048]{1,0:T(8,128)(2,1)}, u32[]{:S(2)}, u32[]{:S(2)}) collective-permute-start(bf16[1024,2048]{1,0:T(8,128)(2,1)} %collective-permute-done), channel_id=1, source_target_pairs={{0,8},{8,16},{16,24},{24,0},{1,9},{9,17},{17,25},{25,1},{2,10},{10... | collective-permute-start | bytes 12582920 | tf_op jit(solution)/shard_map/ppermute | solution.py:17
  128.8 6.8 copy-start
  795.8 4.0 copy-start.1
  795.8 4.0 copy-start.2
  795.8 368.6 %all-to-all-start.1 = ((bf16[512,32,512]{0,2,1:T(8,128)(2,1)}), bf16[512,32,512]{0,2,1:T(8,128)(2,1)}, u32[]{:S(2)}, u32[]{:S(2)}) async-start(bf16[512,32,512]{0,2,1:T(8,128)(2,1)} %bitcast.19), calls=%async_computation.1 | async-start | bytes 33554432 | tf_op jit(solution)/shard_map/all_to_all | solution.py:48
Sparse Core Ops, SparseCore 0:
  32.2 291.3 all-gather.1
